TPU v7x, 32 devices: a whole 2x2x4 slice. The times are simulated.
32 devices in a mesh: dp: 4 (over x, core), seq: 8 (over z, y).
Axes of the slice: x: 2, y: 2, z: 4, core: 2. Of those that a mesh axis runs over, the one named last changes fastest.
Arguments:
- tokens: bfloat16 [32768, 1152], P(('dp', 'seq')), may hold values from -6 to 6
- condition: bfloat16 [128, 1152], P('dp'), may hold values from -6 to 6
- lengths: int32 [128], P(('dp', 'seq')), may hold values from 1 to 256, 22937 in all
- kept_index: int32 [128, 256], P(('dp', 'seq')), may hold values from 0 to 255, each once within a row
- heads_weight: bfloat16 [1152, 3456], P('seq'), may hold values from -0.1875 to 0.1875
- heads_bias: bfloat16 [2304], replicated, may hold values from -1.5 to 1.5
- merge_weight: bfloat16 [1152, 1152], P('seq'), may hold values from -1.5 to 1.5
- merge_bias: bfloat16 [1152], replicated, may hold values from -4 to 4
- up_weight: bfloat16 [1152, 4608], P('seq'), may hold values from -0.1875 to 0.1875
- up_bias: bfloat16 [4608], replicated, may hold values from -4 to 4
- down_weight: bfloat16 [1152, 4608], P('seq'), may hold values from -0.1875 to 0.1875
- down_bias: bfloat16 [1152], replicated, may hold values from -4 to 4
- modulate_weight: bfloat16 [1152, 6912], P('seq'), may hold values from -0.1875 to 0.1875
- modulate_bias: bfloat16 [6912], replicated, may hold values from -4 to 4
- relative_table: bfloat16 [16, 961], replicated, may hold values from -6 to 6
- cotangent: bfloat16 [32768, 1152], P(('dp', 'seq')), may hold values from -6 to 6
Outputs:
- output: bfloat16 [32768, 1152], P(('dp', 'seq'))
- tokens_grad: float32 [32768, 1152], P(('dp', 'seq'))
- heads_weight_grad: float32 [1152, 3456], P('seq')
- merge_weight_grad: float32 [1152, 1152], P('seq')
- up_weight_grad: float32 [1152, 4608], P('seq')
- down_weight_grad: float32 [1152, 4608], P('seq')
- modulate_weight_grad: float32 [1152, 6912], P('seq')
- heads_bias_grad: float32 [2304], replicated
- merge_bias_grad: float32 [1152], replicated
- up_bias_grad: float32 [4608], replicated
- down_bias_grad: float32 [1152], replicated
- modulate_bias_grad: float32 [6912], replicated
- relative_table_grad: float32 [16, 961], replicated
Inputs may be any that keep to these rules, and one draw needn't show every extreme that they name: The first lengths[s] slots of sample s hold its kept tokens, the rest are empty. Each sample's row is a permutation of the 256 patch positions; slot r's patch lies at row kept_index // 16, column kept_index % 16.
All inputs are finite; a program needn't handle non-finite values. No bound on the sum of `lengths` on one device may be relied on, other than what follows from the above.
Results may differ from a plain program's by a relative error of at most 0.019.
Values may be sent and summed in bfloat16 or wider, within the bound.
No kernel may reach another device: no remote copies, remote signals or barrier semaphores. Data moves between devices by JAX's collectives and lax.ppermute only.
A program may use at most 320 MiB of HBM per device.

v0:
```python
from functools import partial
import math
import jax
import jax.numpy as jnp
from jax import lax
from jax.sharding import PartitionSpec as P

D = 1152
HEADS = 16
HEAD = 72
FF = 4608
SIDE = 16
MICRO = 2
SAMP_DEV = 4
GRID = 256
epsilon = 1e-06


def layer_norm(values):
    center = values - jnp.mean(values, axis=-1, keepdims=True)
    spread = jnp.mean(center * center, axis=-1, keepdims=True)
    return center * lax.rsqrt(spread + epsilon)


def modulated(values, scales, shifts):
    return layer_norm(values) * (1.0 + scales) + shifts


def gelu_tanh(values):
    return jax.nn.gelu(values, approximate=True)


def fold_rows(left, portion):
    return jnp.dot(left, portion, preferred_element_type=jnp.float32)


def right_transposed(left, portion):
    return lax.dot_general(
        left, portion, (((1,), (1,)), ((), ())), preferred_element_type=jnp.float32
    )


def column_outer(left, right):
    return lax.dot_general(
        left, right, (((0,), (0,)), ((), ())), preferred_element_type=jnp.float32
    )


def relative_index(positions):
    row_place = positions // SIDE
    col_place = positions % SIDE
    row_gap = row_place[..., :, None] - row_place[..., None, :] + (SIDE - 1)
    col_gap = col_place[..., :, None] - col_place[..., None, :] + (SIDE - 1)
    return row_gap * (2 * SIDE - 1) + col_gap


def slot_onehot(index_pair):
    return (index_pair[..., :, None] == jnp.arange(GRID)[None, None, :]).astype(jnp.bfloat16)


def pair_scores(packed, lens_pair, index_pair, position_bias):
    parts = packed.reshape(2, GRID, 3, HEADS, HEAD)
    queries = parts[:, :, 0]
    key_part = parts[:, :, 1]
    value_part = parts[:, :, 2]
    scaling = 1.0 / math.sqrt(HEAD)
    onehot = slot_onehot(index_pair)
    rows_placed = jnp.einsum(
        "srp,hpq->hsrq", onehot, position_bias, preferred_element_type=jnp.float32
    ).astype(jnp.bfloat16)
    bias_pair = jnp.einsum(
        "hsrq,skq->hsrk", rows_placed, onehot, preferred_element_type=jnp.float32
    )
    scores = (
        jnp.einsum("sqhe,skhe->hsqk", queries, key_part, preferred_element_type=jnp.float32)
        * scaling
    )
    scores = scores + bias_pair
    living = jnp.arange(GRID)[None, :] < lens_pair[:, None]
    scores = jnp.where(living[None, :, None, :], scores, -1e30)
    return (scores, queries, key_part, value_part, onehot)


def attend_pair(arguments, position_bias):
    packed, lens_pair, index_pair = arguments
    scores, queries, key_part, value_part, onehot = pair_scores(
        packed, lens_pair, index_pair, position_bias
    )
    peak = jnp.max(scores, axis=-1, keepdims=True)
    expo = jnp.exp(scores - peak)
    mass = jnp.sum(expo, axis=-1, keepdims=True)
    probs_low = (expo / mass).astype(jnp.bfloat16)
    mixed = jnp.einsum("hsqk,skhe->sqhe", probs_low, value_part, preferred_element_type=jnp.float32)
    return (mixed.astype(jnp.bfloat16).reshape(2 * GRID, D), (peak + jnp.log(mass))[..., 0])


def attend_pair_back(arguments, position_bias):
    packed, lens_pair, index_pair, logsum, grad_mixed = arguments
    scores, queries, key_part, value_part, onehot = pair_scores(
        packed, lens_pair, index_pair, position_bias
    )
    probs = jnp.exp(scores - logsum[..., None])
    grad_mixed = grad_mixed.reshape(2, GRID, HEADS, HEAD)
    grad_probs = jnp.einsum(
        "sqhe,skhe->hsqk", grad_mixed, value_part, preferred_element_type=jnp.float32
    )
    inner = jnp.sum(probs * grad_probs, axis=-1, keepdims=True)
    grad_scores = (probs * (grad_probs - inner)).astype(jnp.bfloat16)
    scaling = 1.0 / math.sqrt(HEAD)
    grad_query = (
        jnp.einsum("hsqk,skhe->sqhe", grad_scores, key_part, preferred_element_type=jnp.float32)
        * scaling
    )
    grad_key = (
        jnp.einsum("hsqk,sqhe->skhe", grad_scores, queries, preferred_element_type=jnp.float32)
        * scaling
    )
    grad_value = jnp.einsum(
        "hsqk,sqhe->skhe",
        probs.astype(jnp.bfloat16),
        grad_mixed,
        preferred_element_type=jnp.float32,
    )
    stacked = (
        jnp.stack([grad_query, grad_key, grad_value], axis=2)
        .astype(jnp.bfloat16)
        .reshape(2 * GRID, 3 * D)
    )
    rows_back = jnp.einsum(
        "hsrk,srp->hspk", grad_scores, onehot, preferred_element_type=jnp.float32
    ).astype(jnp.bfloat16)
    placed_grad = jnp.einsum("hspk,skq->hpq", rows_back, onehot, preferred_element_type=jnp.float32)
    return (stacked, placed_grad)


def offsets_table(placed_grad):
    spots = jnp.arange(SIDE)
    reach = jnp.arange(2 * SIDE - 1)
    gaps = (
        spots[:, None, None] - spots[None, :, None] + (SIDE - 1) == reach[None, None, :]
    ).astype(jnp.float32)
    grid_grad = placed_grad.reshape(HEADS, SIDE, SIDE, SIDE, SIDE)
    by_rows = jnp.einsum("hwxyz,wya->haxz", grid_grad, gaps, precision=lax.Precision.HIGHEST)
    return jnp.einsum("haxz,xzb->hab", by_rows, gaps, precision=lax.Precision.HIGHEST).reshape(
        HEADS, (2 * SIDE - 1) ** 2
    )


def local(
    tokens,
    condition,
    lengths,
    kept_index,
    heads_weight,
    heads_bias,
    merge_weight,
    merge_bias,
    up_weight,
    up_bias,
    down_weight,
    down_bias,
    modulate_weight,
    modulate_bias,
    relative_table,
    cotangent,
):
    position = lax.axis_index("seq")
    position_bias = jnp.take(relative_table, relative_index(jnp.arange(GRID)), axis=1)
    own_cond = lax.dynamic_slice_in_dim(condition, position * SAMP_DEV, SAMP_DEV, 0)
    own_silu = jax.nn.silu(own_cond.astype(jnp.float32)).astype(jnp.bfloat16)
    modulation = fold_rows(own_silu, lax.all_gather(modulate_weight, "seq", axis=0, tiled=True))
    modulation = (modulation + modulate_bias.astype(jnp.float32)).reshape(SAMP_DEV, 1, 6, D)
    full_bias = jnp.concatenate(
        [heads_bias[:D], jnp.zeros((D,), jnp.bfloat16), heads_bias[D:]]
    ).astype(jnp.float32)
    parts_count = MICRO
    samples = SAMP_DEV // parts_count
    rows = samples * GRID
    pairs = samples // 2
    kept = {
        "out": [],
        "tgrad": [],
        "mgrad": [],
        "hone": [],
        "gpack": [],
        "attn": [],
        "gbranch": [],
        "htwo": [],
        "gup": [],
        "gmlp": [],
        "act": [],
    }
    placed_total = jnp.zeros((HEADS, GRID, GRID), jnp.float32)
    for part in range(parts_count):
        slab = tokens[part * rows : (part + 1) * rows].astype(jnp.float32).reshape(samples, GRID, D)
        mods = modulation[part * samples : (part + 1) * samples]
        shift_one, scale_one, gate_one, shift_two, scale_two, gate_two = [
            mods[:, :, index] for index in range(6)
        ]
        lens_part = lengths[part * samples : (part + 1) * samples]
        index_part = kept_index[part * samples : (part + 1) * samples]
        living = (jnp.arange(GRID)[None, :] < lens_part[:, None])[:, :, None]
        hidden_one = modulated(slab, scale_one, shift_one).astype(jnp.bfloat16).reshape(rows, D)
        packed = (
            fold_rows(hidden_one, lax.all_gather(heads_weight, "seq", axis=0, tiled=True))
            + full_bias
        ).astype(jnp.bfloat16)
        packed_pairs = packed.reshape(pairs, 2 * GRID, 3 * D)
        lens_pairs = lens_part.reshape(pairs, 2)
        index_pairs = index_part.reshape(pairs, 2, GRID)
        attended, logsum = lax.map(
            partial(attend_pair, position_bias=position_bias),
            (packed_pairs, lens_pairs, index_pairs),
        )
        attended = attended.reshape(rows, D)
        branch = fold_rows(
            attended, lax.all_gather(merge_weight, "seq", axis=0, tiled=True)
        ) + merge_bias.astype(jnp.float32)
        branch = branch.reshape(samples, GRID, D)
        middle = slab + gate_one * branch
        hidden_two = modulated(middle, scale_two, shift_two).astype(jnp.bfloat16).reshape(rows, D)
        up_value = fold_rows(
            hidden_two, lax.all_gather(up_weight, "seq", axis=0, tiled=True)
        ) + up_bias.astype(jnp.float32)
        activated = gelu_tanh(up_value).astype(jnp.bfloat16)
        mlp_out = right_transposed(
            activated, lax.all_gather(down_weight, "seq", axis=0, tiled=True)
        )
        mlp_out = (mlp_out + down_bias.astype(jnp.float32)).reshape(samples, GRID, D)
        final = jnp.where(living, middle + gate_two * mlp_out, 0.0)
        kept["out"].append(final.astype(jnp.bfloat16).reshape(rows, D))
        grad_final = jnp.where(
            living,
            cotangent[part * rows : (part + 1) * rows]
            .astype(jnp.float32)
            .reshape(samples, GRID, D),
            0.0,
        )
        gate_two_grad = jnp.sum(grad_final * mlp_out, axis=1, keepdims=True)
        grad_mlp = (gate_two * grad_final).astype(jnp.bfloat16).reshape(rows, D)
        grad_act = fold_rows(grad_mlp, lax.all_gather(down_weight, "seq", axis=0, tiled=True))
        grad_up = jax.vjp(gelu_tanh, up_value)[1](grad_act)[0].astype(jnp.bfloat16)
        grad_hidden_two = right_transposed(
            grad_up, lax.all_gather(up_weight, "seq", axis=0, tiled=True)
        )
        middle_ln, scale_two_grad, shift_two_grad = jax.vjp(
            modulated, middle, scale_two, shift_two
        )[1](grad_hidden_two.reshape(samples, GRID, D))
        grad_middle = grad_final + middle_ln
        gate_one_grad = jnp.sum(grad_middle * branch, axis=1, keepdims=True)
        grad_branch = (gate_one * grad_middle).astype(jnp.bfloat16).reshape(rows, D)
        grad_attended = right_transposed(
            grad_branch, lax.all_gather(merge_weight, "seq", axis=0, tiled=True)
        ).astype(jnp.bfloat16)
        grad_packed, placed_parts = lax.map(
            partial(attend_pair_back, position_bias=position_bias),
            (
                packed_pairs,
                lens_pairs,
                index_pairs,
                logsum,
                grad_attended.reshape(pairs, 2 * GRID, D),
            ),
        )
        grad_packed = grad_packed.reshape(rows, 3 * D)
        placed_total = placed_total + jnp.sum(placed_parts, axis=0)
        grad_hidden_one = right_transposed(
            grad_packed, lax.all_gather(heads_weight, "seq", axis=0, tiled=True)
        )
        slab_ln, scale_one_grad, shift_one_grad = jax.vjp(modulated, slab, scale_one, shift_one)[1](
            grad_hidden_one.reshape(samples, GRID, D)
        )
        kept["tgrad"].append((grad_middle + slab_ln).reshape(rows, D))
        kept["mgrad"].append(
            jnp.concatenate(
                [
                    shift_one_grad,
                    scale_one_grad,
                    gate_one_grad,
                    shift_two_grad,
                    scale_two_grad,
                    gate_two_grad,
                ],
                axis=-1,
            ).reshape(samples, 6 * D)
        )
        kept["hone"].append(hidden_one)
        kept["gpack"].append(grad_packed)
        kept["attn"].append(attended)
        kept["gbranch"].append(grad_branch)
        kept["htwo"].append(hidden_two)
        kept["gup"].append(grad_up)
        kept["gmlp"].append(grad_mlp)
        kept["act"].append(activated)
    table_grad = offsets_table(placed_total)
    joined = {name: jnp.concatenate(items, axis=0) for name, items in kept.items()}
    mod_grad = joined["mgrad"].astype(jnp.bfloat16)
    pieces = [
        column_outer(joined["hone"], joined["gpack"]),
        column_outer(joined["attn"], joined["gbranch"]),
        column_outer(joined["htwo"], joined["gup"]),
        column_outer(joined["gmlp"], joined["act"]),
        column_outer(own_silu, mod_grad),
    ]
    summed = lax.psum_scatter(
        jnp.concatenate(pieces, axis=1).astype(jnp.bfloat16), "seq", scatter_dimension=0, tiled=True
    )
    share = lax.psum_scatter(summed, "dp", scatter_dimension=0, tiled=True).astype(jnp.float32)
    replicated = lax.all_gather(share.astype(jnp.bfloat16), "dp", axis=0, tiled=True).astype(
        share.dtype
    )
    packed_sums = jnp.sum(joined["gpack"], axis=0, dtype=jnp.float32)
    heads_part = jnp.concatenate([packed_sums[:D], packed_sums[2 * D :]])
    merge_part = jnp.sum(joined["gbranch"], axis=0, dtype=jnp.float32)
    up_part = jnp.sum(joined["gup"], axis=0, dtype=jnp.float32)
    down_part = jnp.sum(joined["gmlp"], axis=0, dtype=jnp.float32)
    modulate_part = jnp.sum(mod_grad, axis=0, dtype=jnp.float32)
    heads_total, merge_total, up_total, down_total, modulate_total, table_total = lax.psum(
        (heads_part, merge_part, up_part, down_part, modulate_part, table_grad), ("dp", "seq")
    )
    edges = [0, 3 * D, 4 * D, 4 * D + FF, 4 * D + 2 * FF, 10 * D + 2 * FF]
    return (
        joined["out"],
        joined["tgrad"],
        replicated[:, edges[0] : edges[1]],
        replicated[:, edges[1] : edges[2]],
        replicated[:, edges[2] : edges[3]],
        replicated[:, edges[3] : edges[4]],
        replicated[:, edges[4] : edges[5]],
        heads_total,
        merge_total,
        up_total,
        down_total,
        modulate_total,
        table_total,
    )


def solution(mesh):
    in_specs = (
        P(("dp", "seq"), None),
        P("dp", None),
        P(("dp", "seq")),
        P(("dp", "seq"), None),
        P("seq", None),
        P(),
        P("seq", None),
        P(),
        P("seq", None),
        P(),
        P("seq", None),
        P(),
        P("seq", None),
        P(),
        P(),
        P(("dp", "seq"), None),
    )
    out_specs = (
        P(("dp", "seq"), None),
        P(("dp", "seq"), None),
        P("seq", None),
        P("seq", None),
        P("seq", None),
        P("seq", None),
        P("seq", None),
        P(),
        P(),
        P(),
        P(),
        P(),
        P(),
    )
    return jax.shard_map(local, mesh=mesh, in_specs=in_specs, out_specs=out_specs, check_vma=False)
```

profile of v0, /device:TPU:8, one launch (start us, length us, event | category | flops | bytes accessed | tf_op | source)
XLA Modules:
  0.0 2067.6 jit_solution(3447131822799105786)
XLA Ops:
  21.8 4.3 slice_convert_fusion.1
  26.2 227.7 %gather_fusion = bf16[65536,16]{1,0:T(8,128)(2,1)} fusion(bf16[16,961]{0,1:T(8,128)(2,1)S(1)} %copy.147, s32[65536]{0:T(1024)S(1)} %broadcast_clamp_fusion), kind=kCustom, calls=%fused_computation | custom fusion | bytes 4456448 | tf_op jit(solution)/shard_map/jit(_take)/gather | solution.py:168
  253.8 16.7 copy.148
  270.6 5.1 convert_bitcast_fusion
  279.7 7.9 convolution_add_fusion
  292.3 54.5 %all-gather.10.cloned.1.call-done = bf16[1152,3456]{1,0:T(8,128)(2,1)} async-done(((bf16[144,3456]{1,0:T(8,128)(2,1)}), bf16[1152,3456]{1,0:T(8,128)(2,1)}) %all-gather.10.cloned.1.call-update) | async-done | bytes 7962640 | tf_op jit(solution)/shard_map/all_gather | solution.py:205
  346.7 9.5 add_convert_fusion.1
  356.3 5.8 copy.143
  362.1 8.3 reshape.859
  370.4 15.9 fusion.217
  399.5 4.5 all-gather.12.cloned.1.call-done
  404.0 6.8 fusion.212
  411.4 11.2 add_convert_fusion
  422.6 5.7 copy.152
  428.3 8.3 reshape.861
  467.8 87.5 %all-gather.14.cloned.1.call-done = bf16[1152,4608]{1,0:T(8,128)(2,1)} async-done(((bf16[144,4608]{1,0:T(8,128)(2,1)}), bf16[1152,4608]{1,0:T(8,128)(2,1)}) %all-gather.14.cloned.1.call-update) | async-done | bytes 10616848 | tf_op jit(solution)/shard_map/all_gather | solution.py:223
  555.3 11.7 fusion.231
  566.9 8.9 fusion.230
  575.8 132.2 %all-gather.16.cloned.1.call-done = bf16[1152,4608]{1,0:T(8,128)(2,1)} async-done(((bf16[144,4608]{1,0:T(8,128)(2,1)}), bf16[1152,4608]{1,0:T(8,128)(2,1)}) %all-gather.16.cloned.1.call-update) | async-done | bytes 10616848 | tf_op jit(solution)/shard_map/all_gather | solution.py:227
  708.0 11.6 fusion.232
  719.6 24.2 %fusion.11 = (bf16[512,4608]{1,0:T(8,128)(2,1)}, bf16[512,4608]{1,0:T(8,128)(2,1)}, bf16[512,4608]{1,0:T(8,128)(2,1)}, bf16[512,4608]{1,0:T(8,128)(2,1)}) fusion(f32[512,4608]{1,0:T(8,128)} %fusion.230, f32[4608]{0:T(1024)S(1)} %copy-done.104, f32[512,4608]{1,0:T(8,128)} %fusion.231, f32[512,4608]{1,0:T(8,128)} %fusion.232, ...), kind=kOutput, calls=%fused_computation.21 | convolution fusion | flops 5544345600 | bytes 59000832 | tf_op jit(solution)/shard_map/dot_general | solution.py:34
  743.8 12.7 multiply_reduce_fusion.11
  757.2 13.2 multiply_reduce_fusion.9
  771.0 14.4 fusion.210
  785.5 13.1 fusion.211
  810.9 5.3 multiply_reduce_fusion.1
  832.8 4.8 convolution_convert_fusion.4
  847.4 6.1 multiply_reduce_fusion
  864.9 5.5 copy.182
  874.3 5.2 copy.183
  883.6 8.8 multiply_reduce_fusion.10
  899.8 10.3 multiply_reduce_fusion.8
  910.2 4.8 multiply_reduce_fusion.4
  916.6 10.9 fusion.4
  931.0 17.3 fusion.3
  948.4 16.6 fusion.2
  975.5 8.7 fusion.1
  984.2 748.7 %reduce-scatter.4.cloned.1.call-done = bf16[144,20736]{1,0:T(8,128)(2,1)} async-done(((bf16[1152,20736]{1,0:T(8,128)(2,1)}), bf16[144,20736]{1,0:T(8,128)(2,1)}) %reduce-scatter.4.cloned.1.call-update) | async-done | bytes 5971984 | tf_op jit(solution)/shard_map/reduce_scatter | solution.py:305
  1732.9 62.0 %fusion = bf16[40,20736]{1,0:T(8,128)(2,1)} fusion(bf16[144,20736]{1,0:T(8,128)(2,1)} %reduce-scatter.4.cloned.1.call-done), kind=kCustom, calls=%all-reduce-scatter | all-reduce-scatter fusion | flops 3317761 | bytes 7631360
  1800.4 17.0 concatenate.72
  1820.6 6.8 fusion.32
  1827.4 8.1 bitcast_add_fusion.2
  1835.4 19.8 add.547
  1855.2 33.3 %fusion.185 = f32[31,16,16,16,1]{0,3,2,4,1:T(8,128)} fusion(f32[16,16,16,16,16]{4,3,2,1,0:T(8,128)} %add.547, s32[16,16]{1,0:T(8,128)S(1)} %subtract_add_fusion), kind=kOutput, calls=%fused_computation.258 | convolution fusion | flops 390078208 | bytes 4703232 | tf_op jit(solution)/shard_map/hwxyz,wya->haxz/dot_general | solution.py:143
  1911.9 4.3 convert_reduce_fusion
  1916.3 10.3 reshape.899
  1926.6 5.7 fusion.216
  1938.7 113.8 %all-reduce.5.cloned.1.call-done = (f32[2304]{0:T(1024)}, f32[1152]{0:T(1024)}, f32[4608]{0:T(1024)}, f32[1152]{0:T(1024)}, f32[6912]{0:T(1024)}, /*index=5*/f32[16,961]{1,0:T(8,128)}) async-done(((f32[2304]{0:T(1024)}, f32[1152]{0:T(1024)}, f32[4608]{0:T(1024)}, f32[1152]{0:T(1024)}, f32[6912]{0:T(1024)}, /*index=5*/f32[16,961]{1,0:T(8,128)}), (f32[2304]{0:T(1024)}, f32[1152]{0:T(1024)}, f32[4608]{0:T(1024)}, ...) | async-done | bytes 126032 | tf_op jit(solution)/shard_map/psum | solution.py:318
  (496 shorter events, 194.9 us)
Async XLA Ops:
  7.2 272.5 %all-gather.8.cloned.1.call-start = ((), (), s32[]{:S(2)}) async-start(), calls=%async_computation.1 | async-start | bytes 17915904 | tf_op jit(solution)/shard_map/all_gather | solution.py:171
  7.9 338.8 %all-gather.10.cloned.1.call-start = ((), (), s32[]{:S(2)}) async-start(), calls=%async_computation.2 | async-start | bytes 8957952 | tf_op jit(solution)/shard_map/all_gather | solution.py:205
  8.7 395.3 %all-gather.12.cloned.1.call-start = ((), (), s32[]{:S(2)}) async-start(), calls=%async_computation.3 | async-start | bytes 2985984 | tf_op jit(solution)/shard_map/all_gather | solution.py:217
  9.4 545.9 %all-gather.14.cloned.1.call-start = ((), (), s32[]{:S(2)}) async-start(), calls=%async_computation.4 | async-start | bytes 11943936 | tf_op jit(solution)/shard_map/all_gather | solution.py:223
  10.0 698.0 %all-gather.16.cloned.1.call-start = ((), (), s32[]{:S(2)}) async-start(), calls=%async_computation.5 | async-start | bytes 11943936 | tf_op jit(solution)/shard_map/all_gather | solution.py:227
  10.6 1722.4 %reduce-scatter.4.cloned.1.call-start = ((), (), s32[]{:S(2)}) async-start(), calls=%async_computation.6 | async-start | bytes 53747712 | tf_op jit(solution)/shard_map/reduce_scatter | solution.py:305
  17.2 253.4 %copy-start.135 = (s32[2,256]{1,0:T(2,128)}, s32[2,256]{1,0:T(2,128)S(1)}, u32[]{:S(2)}) copy-start(s32[2,256]{1,0:T(2,128)S(1)} %get-tuple-element.193) | copy-start | bytes 6148
  17.2 370.5 %copy-start.98 = (s32[2,256]{1,0:T(2,128)}, s32[2,256]{1,0:T(2,128)S(1)}, u32[]{:S(2)}) copy-start(s32[2,256]{1,0:T(2,128)S(1)} %get-tuple-element.192) | copy-start | bytes 6148
  292.3 64.0 %copy-start.63 = (bf16[512,1152]{1,0:T(8,128)(2,1)}, bf16[512,1152]{1,0:T(8,128)(2,1)S(1)}, u32[]{:S(2)}) copy-start(bf16[512,1152]{1,0:T(8,128)(2,1)S(1)} %fusion.98) | copy-start | bytes 3538948
  398.8 12.0 copy-start.54
  399.5 11.3 copy-start.70
  461.2 309.8 %copy-start.74 = (f32[2,1152]{1,0:T(2,128)}, f32[2,1152]{1,0:T(2,128)S(1)}, u32[]{:S(2)}) copy-start(f32[2,1152]{1,0:T(2,128)S(1)} %get-tuple-element.239) | copy-start | bytes 27652
  464.0 321.5 %copy-start.81 = (f32[2,1152]{1,0:T(2,128)}, f32[2,1152]{1,0:T(2,128)S(1)}, u32[]{:S(2)}) copy-start(f32[2,1152]{1,0:T(2,128)S(1)} %get-tuple-element.235) | copy-start | bytes 27652
  555.3 11.7 copy-start.66
  555.3 11.7 copy-start.155
  708.0 11.6 copy-start.5
  708.0 11.6 copy-start.104
  757.2 13.2 copy-start.110
  757.2 13.8 copy-start.88
  757.2 13.8 copy-start.108
  757.2 13.8 copy-start.149
  771.0 14.5 copy-start.10
  771.0 14.5 copy-start.11
  771.0 14.5 copy-start.106
  771.0 14.5 copy-start.147
  785.5 14.2 copy-start.71
  883.5 8.9 copy-start.139
  883.5 8.9 copy-start.1
  883.5 8.9 copy-start.13
  883.5 8.9 copy-start.15
  883.6 8.9 copy-start.114
  899.8 10.3 copy-start.138
  899.8 10.4 copy-start.12
  899.8 10.4 copy-start.14
  899.8 10.4 copy-start.73
  899.8 10.4 copy-start.115
  916.6 10.9 copy-start.17
  931.0 17.3 copy-start.52
  948.3 16.7 copy-start.75
  948.3 16.7 copy-start.126
  948.3 16.7 copy-start.134
  984.2 815.0 %copy-start.154 = (u32[32]{0:T(128)S(1)}, u32[32]{0:T(128)}, u32[]{:S(2)}) copy-start(u32[32]{0:T(128)} %constant.195) | copy-start | bytes 388
  984.2 932.1 %all-gather.18.cloned.1.call-start = ((), (), s32[]{:S(2)}) async-start(), calls=%async_computation.7 | async-start | bytes 8294400 | tf_op jit(solution)/shard_map/all_gather | solution.py:309
  1797.0 3.4 collective-permute-start
  1820.5 232.0 %all-reduce.5.cloned.1.call-start = ((), (), s32[]{:S(2)}) async-start(), calls=%async_computation.8 | async-start | bytes 286720 | tf_op jit(solution)/shard_map/psum | solution.py:318
  1896.0 8.5 copy-start.77
  1896.0 8.5 copy-start.80
  1926.6 8.5 copy-start.4
  (123 other events, 456.9 us)
Sparse Core Ops, SparseCore 0:
  10.2 216.5 all-gather.7
  228.9 117.7 all-gather.9
  348.9 55.0 all-gather.11
  406.0 149.1 all-gather.13
  557.3 150.6 all-gather.15
  984.3 748.6 reduce-scatter.3
  1820.6 57.1 all-gather.17
  1916.3 136.0 all-reduce.4
where the time goes:
time: 2070 us
  waiting for transfers between devices  1140 us (55%)
  local copies, waits for them, and re-layouts  442 us (21%)
  matrix products  327 us (16%)
  other arithmetic  72.9 us (4%)
  blocking collectives  62 us (3%)
    reduce_scatter x1, waiting for transfers between devices, local(): lax.psum_scatter(jnp.concatenate(pieces, axis=1).astype(jnp.bfloat16), 's...  749 us
    gather x2, local copies, waits for them, and re-layouts, local(): jnp.take(relative_table, relative_index(jnp.arange(GRID)), axis=1)  244 us
    all_gather x1, waiting for transfers between devices, local(): lax.all_gather(down_weight, 'seq', axis=0, tiled=True)  132 us
    psum x1, waiting for transfers between devices, local(): lax.psum((heads_part, merge_part, up_part, down_part, modulate_part, tabl...  114 us
    dot_general x9, matrix products, fold_rows(): return jnp.dot(left, portion, preferred_element_type=jnp.float32)  96.1 us
    all_gather x1, waiting for transfers between devices, local(): lax.all_gather(up_weight, 'seq', axis=0, tiled=True)  87.5 us
    dot_general x8, matrix products, right_transposed(): lax.dot_general(left, portion, (((1,), (1,)), ((), ())), preferred_elemen...  77.3 us
    unnamed x359, local copies, waits for them, and re-layouts  65.2 us
  transfers between devices with their start and end apart: 9, of which 6 were waited for; matrix products, arithmetic and copies ran while one was open for 25% of the time, Pallas kernels for 0%

commit v1 on v0

--- a/solution.py
+++ b/solution.py
@@ -164,6 +164,11 @@
     relative_table,
     cotangent,
 ):
+
+    def local_data_convert(array_here):
+        near = lax.psum(lax.psum(array_here, "seq"), "dp")
+        return near
+
     position = lax.axis_index("seq")
     position_bias = jnp.take(relative_table, relative_index(jnp.arange(GRID)), axis=1)
     own_cond = lax.dynamic_slice_in_dim(condition, position * SAMP_DEV, SAMP_DEV, 0)
@@ -315,8 +320,8 @@
     up_part = jnp.sum(joined["gup"], axis=0, dtype=jnp.float32)
     down_part = jnp.sum(joined["gmlp"], axis=0, dtype=jnp.float32)
     modulate_part = jnp.sum(mod_grad, axis=0, dtype=jnp.float32)
-    heads_total, merge_total, up_total, down_total, modulate_total, table_total = lax.psum(
-        (heads_part, merge_part, up_part, down_part, modulate_part, table_grad), ("dp", "seq")
+    heads_total, merge_total, up_total, down_total, modulate_total, table_total = (
+        local_data_convert((heads_part, merge_part, up_part, down_part, modulate_part, table_grad))
     )
     edges = [0, 3 * D, 4 * D, 4 * D + FF, 4 * D + 2 * FF, 10 * D + 2 * FF]
     return (

time: 2070 us -> 1980 us (0.957)
  waiting for transfers between devices: 1140 us -> 1050 us
    reduce_scatter x1, waiting for transfers between devices: 749 us -> 668 us  [local(): lax.psum_scatter(jnp.concatenate(pieces, axis=1).astype(jnp.bfloat16), 's...]
    psum x1 -> x2, waiting for transfers between devices: 114 us -> 54.7 us  [local_data_convert(): near = lax.psum(lax.psum(array_here, 'seq'), 'dp')]
    all_gather x1, waiting for transfers between devices: 0.02 us -> 50.5 us  [local(): lax.all_gather(share.astype(jnp.bfloat16), 'dp', axis=0, tiled=True)]
    unnamed x359 -> x337, local copies, waits for them, and re-layouts: 65.2 us -> 61.1 us
  transfers between devices with their start and end apart: 9 -> 10, of which waited for: 6 -> 8; matrix products, arithmetic and copies ran while one was open for 25% -> 28% of each run, Pallas kernels for 0% -> 0%
where the time goes in v1:
time: 1980 us
  waiting for transfers between devices  1050 us (53%)
  local copies, waits for them, and re-layouts  439 us (22%)
  matrix products  326 us (16%)
  other arithmetic  79.3 us (4%)
  blocking collectives  61.9 us (3%)
    reduce_scatter x1, waiting for transfers between devices, local(): lax.psum_scatter(jnp.concatenate(pieces, axis=1).astype(jnp.bfloat16), 's...  668 us
    gather x2, local copies, waits for them, and re-layouts, local(): jnp.take(relative_table, relative_index(jnp.arange(GRID)), axis=1)  246 us
    all_gather x1, waiting for transfers between devices, local(): lax.all_gather(down_weight, 'seq', axis=0, tiled=True)  132 us
    dot_general x9, matrix products, fold_rows(): return jnp.dot(left, portion, preferred_element_type=jnp.float32)  95.9 us
    all_gather x1, waiting for transfers between devices, local(): lax.all_gather(up_weight, 'seq', axis=0, tiled=True)  87.5 us
    dot_general x8, matrix products, right_transposed(): lax.dot_general(left, portion, (((1,), (1,)), ((), ())), preferred_elemen...  77.2 us
    unnamed x1, blocking collectives  61.9 us
    unnamed x337, local copies, waits for them, and re-layouts  61.1 us
  transfers between devices with their start and end apart: 10, of which 8 were waited for; matrix products, arithmetic and copies ran while one was open for 28% of the time, Pallas kernels for 0%

profile of v1, /device:TPU:8, one launch (start us, length us, event | category | flops | bytes accessed | tf_op | source)
XLA Modules:
  0.0 1976.9 jit_solution(18083044827375722875)
XLA Ops:
  26.3 229.3 %gather_fusion = bf16[65536,16]{1,0:T(8,128)(2,1)} fusion(bf16[16,961]{0,1:T(8,128)(2,1)S(1)} %copy.147, s32[65536]{0:T(1024)S(1)} %broadcast_clamp_fusion), kind=kCustom, calls=%fused_computation | custom fusion | bytes 4456448 | tf_op jit(solution)/shard_map/jit(_take)/gather | solution.py:173
  255.7 16.7 copy.148
  272.4 5.1 convert_bitcast_fusion
  281.5 7.8 convolution_add_fusion
  294.0 52.8 %all-gather.10.cloned.1.call-done = bf16[1152,3456]{1,0:T(8,128)(2,1)} async-done(((bf16[144,3456]{1,0:T(8,128)(2,1)}), bf16[1152,3456]{1,0:T(8,128)(2,1)}) %all-gather.10.cloned.1.call-update) | async-done | bytes 7962640 | tf_op jit(solution)/shard_map/all_gather | solution.py:210
  346.7 9.5 add_convert_fusion.1
  356.3 5.8 copy.143
  362.1 8.3 reshape.859
  370.4 15.9 fusion.217
  404.0 6.8 fusion.212
  411.4 11.2 add_convert_fusion
  422.6 5.7 copy.152
  428.4 8.3 reshape.861
  467.8 87.5 %all-gather.14.cloned.1.call-done = bf16[1152,4608]{1,0:T(8,128)(2,1)} async-done(((bf16[144,4608]{1,0:T(8,128)(2,1)}), bf16[1152,4608]{1,0:T(8,128)(2,1)}) %all-gather.14.cloned.1.call-update) | async-done | bytes 10616848 | tf_op jit(solution)/shard_map/all_gather | solution.py:228
  555.3 11.7 fusion.231
  566.9 8.9 fusion.230
  575.8 132.2 %all-gather.16.cloned.1.call-done = bf16[1152,4608]{1,0:T(8,128)(2,1)} async-done(((bf16[144,4608]{1,0:T(8,128)(2,1)}), bf16[1152,4608]{1,0:T(8,128)(2,1)}) %all-gather.16.cloned.1.call-update) | async-done | bytes 10616848 | tf_op jit(solution)/shard_map/all_gather | solution.py:232
  708.0 11.6 fusion.232
  719.6 24.2 %fusion.11 = (bf16[512,4608]{1,0:T(8,128)(2,1)}, bf16[512,4608]{1,0:T(8,128)(2,1)}, bf16[512,4608]{1,0:T(8,128)(2,1)}, bf16[512,4608]{1,0:T(8,128)(2,1)}) fusion(f32[512,4608]{1,0:T(8,128)} %fusion.230, f32[4608]{0:T(1024)S(1)} %copy-done.101, f32[512,4608]{1,0:T(8,128)} %fusion.231, f32[512,4608]{1,0:T(8,128)} %fusion.232, ...), kind=kOutput, calls=%fused_computation.21 | convolution fusion | flops 5544345600 | bytes 59000832 | tf_op jit(solution)/shard_map/dot_general | solution.py:34
  743.8 12.7 multiply_reduce_fusion.11
  757.1 13.1 multiply_reduce_fusion.9
  770.9 14.4 fusion.210
  785.4 13.1 fusion.211
  810.8 5.1 multiply_reduce_fusion.1
  832.7 4.8 convolution_convert_fusion.4
  847.3 6.1 multiply_reduce_fusion
  864.7 5.4 copy.182
  874.0 5.2 copy.183
  883.3 8.8 multiply_reduce_fusion.10
  899.6 10.3 multiply_reduce_fusion.8
  910.0 4.7 multiply_reduce_fusion.4
  916.4 10.9 fusion.4
  930.8 17.2 fusion.3
  948.1 16.7 fusion.2
  975.2 8.6 fusion.1
  985.8 7.2 fusion.32
  993.0 8.0 bitcast_add_fusion.2
  1001.0 19.6 add.559
  1024.0 33.4 %fusion.185 = f32[31,16,16,16,1]{0,3,2,4,1:T(8,128)} fusion(f32[16,16,16,16,16]{4,3,2,1,0:T(8,128)} %add.559, s32[16,16]{1,0:T(8,128)S(1)} %subtract_add_fusion), kind=kOutput, calls=%fused_computation.258 | convolution fusion | flops 390078208 | bytes 4703232 | tf_op jit(solution)/shard_map/hwxyz,wya->haxz/dot_general | solution.py:143
  1065.0 667.7 %reduce-scatter.4.cloned.1.call-done = bf16[144,20736]{1,0:T(8,128)(2,1)} async-done(((bf16[1152,20736]{1,0:T(8,128)(2,1)}), bf16[144,20736]{1,0:T(8,128)(2,1)}) %reduce-scatter.4.cloned.1.call-update) | async-done | bytes 5971984 | tf_op jit(solution)/shard_map/reduce_scatter | solution.py:310
  1732.6 61.9 %fusion = bf16[40,20736]{1,0:T(8,128)(2,1)} fusion(bf16[144,20736]{1,0:T(8,128)(2,1)} %reduce-scatter.4.cloned.1.call-done), kind=kCustom, calls=%all-reduce-scatter | all-reduce-scatter fusion | flops 3317761 | bytes 7631360
  1800.1 5.7 convert_reduce_fusion
  1805.9 14.9 concatenate.72
  1834.5 43.3 %all-reduce.7.cloned.1.call-done = (f32[2304]{0:T(1024)}, f32[1152]{0:T(1024)}, f32[4608]{0:T(1024)}, f32[1152]{0:T(1024)}, f32[6912]{0:T(1024)}, /*index=5*/f32[16,961]{1,0:T(8,128)}) async-done(((f32[2304]{0:T(1024)}, f32[1152]{0:T(1024)}, f32[4608]{0:T(1024)}, f32[1152]{0:T(1024)}, f32[6912]{0:T(1024)}, /*index=5*/f32[16,961]{1,0:T(8,128)}), (f32[2304]{0:T(1024)}, f32[1152]{0:T(1024)}, f32[4608]{0:T(1024)}, ...) | async-done | bytes 126032 | tf_op jit(solution)/shard_map/psum | solution.py:169
  1877.8 50.5 %all-gather.18.cloned.1.call-done = bf16[4,36,20736]{2,1,0:T(8,128)(2,1)} async-done(((bf16[1,36,20736]{2,1,0:T(8,128)(2,1)}), bf16[4,36,20736]{2,1,0:T(8,128)(2,1)}) %all-gather.18.cloned.1.call-update) | async-done | bytes 5971984 | tf_op jit(solution)/shard_map/all_gather | solution.py:314
  1928.3 10.4 reshape.899
  1938.7 5.8 fusion.216
  1950.8 11.3 all-reduce.9.cloned.1.call-done
  (476 shorter events, 204.3 us)
Async XLA Ops:
  7.2 274.3 %all-gather.8.cloned.1.call-start = ((), (), s32[]{:S(2)}) async-start(), calls=%async_computation.1 | async-start | bytes 17915904 | tf_op jit(solution)/shard_map/all_gather | solution.py:176
  7.9 338.8 %all-gather.10.cloned.1.call-start = ((), (), s32[]{:S(2)}) async-start(), calls=%async_computation.2 | async-start | bytes 8957952 | tf_op jit(solution)/shard_map/all_gather | solution.py:210
  8.7 395.3 %all-gather.12.cloned.1.call-start = ((), (), s32[]{:S(2)}) async-start(), calls=%async_computation.3 | async-start | bytes 2985984 | tf_op jit(solution)/shard_map/all_gather | solution.py:222
  9.4 545.9 %all-gather.14.cloned.1.call-start = ((), (), s32[]{:S(2)}) async-start(), calls=%async_computation.4 | async-start | bytes 11943936 | tf_op jit(solution)/shard_map/all_gather | solution.py:228
  10.0 698.0 %all-gather.16.cloned.1.call-start = ((), (), s32[]{:S(2)}) async-start(), calls=%async_computation.5 | async-start | bytes 11943936 | tf_op jit(solution)/shard_map/all_gather | solution.py:232
  10.6 1722.1 %reduce-scatter.4.cloned.1.call-start = ((), (), s32[]{:S(2)}) async-start(), calls=%async_computation.6 | async-start | bytes 53747712 | tf_op jit(solution)/shard_map/reduce_scatter | solution.py:310
  17.3 255.1 %copy-start.128 = (s32[2,256]{1,0:T(2,128)}, s32[2,256]{1,0:T(2,128)S(1)}, u32[]{:S(2)}) copy-start(s32[2,256]{1,0:T(2,128)S(1)} %get-tuple-element.199) | copy-start | bytes 6148
  17.3 370.4 %copy-start.95 = (s32[2,256]{1,0:T(2,128)}, s32[2,256]{1,0:T(2,128)S(1)}, u32[]{:S(2)}) copy-start(s32[2,256]{1,0:T(2,128)S(1)} %get-tuple-element.198) | copy-start | bytes 6148
  293.9 62.3 %copy-start.59 = (bf16[512,1152]{1,0:T(8,128)(2,1)}, bf16[512,1152]{1,0:T(8,128)(2,1)S(1)}, u32[]{:S(2)}) copy-start(bf16[512,1152]{1,0:T(8,128)(2,1)S(1)} %fusion.98) | copy-start | bytes 3538948
  398.8 12.0 copy-start.50
  399.5 11.3 copy-start.66
  461.2 309.6 %copy-start.70 = (f32[2,1152]{1,0:T(2,128)}, f32[2,1152]{1,0:T(2,128)S(1)}, u32[]{:S(2)}) copy-start(f32[2,1152]{1,0:T(2,128)S(1)} %get-tuple-element.245) | copy-start | bytes 27652
  464.0 321.3 %copy-start.76 = (f32[2,1152]{1,0:T(2,128)}, f32[2,1152]{1,0:T(2,128)S(1)}, u32[]{:S(2)}) copy-start(f32[2,1152]{1,0:T(2,128)S(1)} %get-tuple-element.241) | copy-start | bytes 27652
  555.3 11.7 copy-start.62
  555.3 11.7 copy-start.146
  708.0 11.6 copy-start.5
  708.0 11.6 copy-start.101
  757.1 13.1 copy-start.107
  757.1 13.8 copy-start.85
  757.1 13.8 copy-start.105
  757.1 13.8 copy-start.140
  770.9 14.4 copy-start.10
  770.9 14.4 copy-start.11
  770.9 14.4 copy-start.103
  770.9 14.4 copy-start.138
  785.4 14.3 copy-start.67
  883.3 8.9 copy-start.132
  883.3 8.9 copy-start.1
  883.3 8.9 copy-start.13
  883.3 8.9 copy-start.15
  883.3 8.9 copy-start.111
  899.5 10.3 copy-start.131
  899.5 10.4 copy-start.12
  899.5 10.4 copy-start.14
  899.5 10.4 copy-start.69
  899.6 10.4 copy-start.112
  916.4 10.9 copy-start.17
  930.8 17.2 copy-start.49
  948.0 16.7 copy-start.71
  948.0 16.7 copy-start.119
  948.0 16.7 copy-start.127
  983.9 893.9 %all-reduce.7.cloned.1.call-start = ((), (), s32[]{:S(2)}) async-start(), calls=%async_computation.8 | async-start | bytes 286720 | tf_op jit(solution)/shard_map/psum | solution.py:169
  1064.9 734.5 %copy-start.82 = (bf16[2,1,6912]{2,0,1:T(2,128)(2,1)S(1)}, bf16[2,1,6912]{2,0,1:T(2,128)(2,1)}, u32[]{:S(2)}) copy-start(bf16[2,1,6912]{2,0,1:T(2,128)(2,1)} %copy-done.81) | copy-start | bytes 82948
  1064.9 734.4 %copy-start.84 = (bf16[2,1,6912]{2,0,1:T(2,128)(2,1)S(1)}, bf16[2,1,6912]{2,0,1:T(2,128)(2,1)}, u32[]{:S(2)}) copy-start(bf16[2,1,6912]{2,0,1:T(2,128)(2,1)} %copy-done.83) | copy-start | bytes 82948
  1796.7 9.3 collective-permute-start
  1805.9 122.5 %all-gather.18.cloned.1.call-start = ((), (), s32[]{:S(2)}) async-start(), calls=%async_computation.7 | async-start | bytes 8294400 | tf_op jit(solution)/shard_map/all_gather | solution.py:314
  1824.1 138.0 %all-reduce.9.cloned.1.call-start = ((), (), s32[]{:S(2)}) async-start(), calls=%async_computation.9 | async-start | bytes 286720 | tf_op jit(solution)/shard_map/psum | solution.py:169
  1938.7 8.5 copy-start.4
  (113 other events, 411.4 us)
Sparse Core Ops, SparseCore 0:
  10.2 216.5 all-gather.7
  228.9 117.7 all-gather.9
  348.9 55.0 all-gather.11
  406.0 149.1 all-gather.13
  557.3 150.6 all-gather.15
  984.0 748.5 reduce-scatter.3
  1806.0 71.7 all-reduce.6
  1880.0 48.2 all-gather.17
  1931.3 30.7 all-reduce.8
